TPU v7x, 32 devices: a whole 2x2x4 slice. The times are simulated.
32 devices in a mesh: tgt: 4 (over y, x), sup: 8 (over z, core).
Axes of the slice: x: 2, y: 2, z: 4, core: 2. Of those that a mesh axis runs over, the one named last changes fastest.
Arguments:
- support: float32 [32, 3, 1024], P(('sup', 'tgt')), may hold values from -14 to 14
- coeffs: float32 [32, 100], P('sup'), may hold values from -10 to 10
- targets: float32 [32, 3, 1024], P(('tgt', 'sup')), may hold values from -14 to 14
- labels: float32 [32, 100], P(('tgt', 'sup')), may hold values from -5 to 5
Outputs:
- support_grad: float32 [32, 3, 1024], P(('sup', 'tgt'))
- residual: float32 [32, 100], P(('tgt', 'sup'))
All inputs are finite; a program needn't handle non-finite values.
Results may differ from a plain program's by a relative error of at most 0.000064.
Values sent between devices are 32-bit elements; how exact they have to be, the bound alone decides.
No kernel may reach another device: no remote copies, remote signals or barrier semaphores. Data moves between devices by JAX's collectives and lax.ppermute only.
A program may use at most 128 MiB of HBM per device.

v0:
```python
import math
import jax
import jax.numpy as jnp
from jax import lax
from jax.sharding import PartitionSpec as P

SIDE = 32
DEPTH = 3
WEIGHT_VAR = 1.6
BIAS_VAR = 0.1


def spread(values):
    side_cells = values.shape[0]
    padded = jnp.pad(values, ((1, 1), (1, 1), (0, 0)))
    summed = jnp.zeros_like(values)
    for row_shift in range(3):
        for col_shift in range(3):
            summed = (
                summed
                + padded[row_shift : row_shift + side_cells, col_shift : col_shift + side_cells]
            )
    return summed / 9.0


def self_levels(images):
    image_count = images.shape[0]
    energy = jnp.mean(images * images, axis=1)
    kernel_level = WEIGHT_VAR * spread(energy.T.reshape(SIDE, SIDE, image_count)) + BIAS_VAR
    levels = [kernel_level]
    for layer_idx in range(DEPTH - 1):
        activated = 2.0 / math.pi * jnp.arcsin(2.0 * kernel_level / (1.0 + 2.0 * kernel_level))
        kernel_level = WEIGHT_VAR * spread(activated) + BIAS_VAR
        levels.append(kernel_level)
    return levels


def pair_kernel(support, targets):
    sup_count = support.shape[0]
    tgt_count = targets.shape[0]
    sup_levels = self_levels(support)
    tgt_levels = self_levels(targets)
    products = (
        jnp.einsum("scp,tcp->pst", support, targets, precision=lax.Precision.HIGHEST)
        / support.shape[1]
    )
    kernel_level = (
        WEIGHT_VAR * spread(products.reshape(SIDE, SIDE, sup_count * tgt_count)) + BIAS_VAR
    )
    activated = kernel_level
    for layer_idx in range(DEPTH):
        sup_gain = lax.rsqrt(1.0 + 2.0 * sup_levels[layer_idx])
        tgt_gain = lax.rsqrt(1.0 + 2.0 * tgt_levels[layer_idx])
        correlation = (
            2.0
            * kernel_level.reshape(SIDE, SIDE, sup_count, tgt_count)
            * sup_gain[:, :, :, None]
            * tgt_gain[:, :, None, :]
        )
        activated = 2.0 / math.pi * jnp.arcsin(correlation)
        if layer_idx + 1 < DEPTH:
            kernel_level = (
                WEIGHT_VAR * spread(activated.reshape(SIDE, SIDE, sup_count * tgt_count)) + BIAS_VAR
            )
    return WEIGHT_VAR * jnp.mean(activated, axis=(0, 1)) + BIAS_VAR


def product(left, right):
    return jnp.dot(left, right, precision=lax.Precision.HIGHEST, preferred_element_type=jnp.float32)


def local(support, coeffs, targets, labels):
    tgt_dev = targets.shape[0]
    block = lax.all_gather(support, "tgt", axis=0, tiled=True)
    group, group_labels = (
        lax.all_gather(targets, "sup", axis=0, tiled=True),
        lax.all_gather(labels, "sup", axis=0, tiled=True),
    )
    theta, pullback = jax.vjp(lambda images: pair_kernel(images, group), block)
    predicted = lax.psum(product(theta.T, coeffs), "sup")
    misfit = predicted - group_labels
    residual = lax.dynamic_slice_in_dim(misfit, lax.axis_index("sup") * tgt_dev, tgt_dev, 0)
    block_grad = pullback(product(coeffs, misfit.T))[0]
    support_grad = lax.psum_scatter(block_grad, "tgt", scatter_dimension=0, tiled=True)
    return (support_grad, residual)


def solution(mesh):
    return jax.shard_map(
        local,
        mesh=mesh,
        in_specs=(
            P(("sup", "tgt"), None, None),
            P("sup", None),
            P(("tgt", "sup"), None, None),
            P(("tgt", "sup"), None),
        ),
        out_specs=(P(("sup", "tgt"), None, None), P(("tgt", "sup"), None)),
        check_vma=False,
    )
```

profile of v0, /device:TPU:0, one launch (start us, length us, event | category | flops | bytes accessed | tf_op | source)
XLA Modules:
  0.0 127.9 jit_solution(11291109133535098446)
XLA Ops:
  0.7 0.7 copy.146
  1.4 9.7 %all_gather.9 = f32[4,3,1024]{2,1,0:T(4,128)S(1)} all-gather(f32[1,3,1024]{2,1,0:T(4,128)S(1)} %copy.146), channel_id=1, replica_groups=mesh['tgt'=4,'sup'=8] {'tgt'}, dimensions={0}, use_global_device_ids=true | all-gather | bytes 61440 | tf_op jit(solution)/shard_map/all_gather | solution.py:74
  11.1 0.2 copy.196
  11.4 0.3 copy.194
  11.7 0.2 broadcast_multiply_fusion.4
  12.0 14.3 %all_gather.10 = f32[8,3,1024]{2,1,0:T(4,128)S(1)} all-gather(f32[1,3,1024]{2,1,0:T(4,128)S(1)} %copy.147), channel_id=1, replica_groups=mesh['tgt'=4,'sup'=8] {'sup'}, dimensions={0}, use_global_device_ids=true | all-gather | bytes 110592 | tf_op jit(solution)/shard_map/all_gather | solution.py:76
  26.3 0.2 copy.197
  26.6 0.2 copy.195
  26.8 0.9 add_rsqrt_fusion.1
  27.8 0.1 broadcast_bitcast_fusion.7
  27.9 2.7 %copy.149 = f32[8,3,1024]{1,0,2:T(8,128)} copy(f32[8,3,1024]{2,1,0:T(4,128)S(1)} %all_gather.10) | data formatting | bytes 196608 | tf_op jit(solution)/shard_map/all_gather | solution.py:76
  30.6 1.8 %copy.148 = f32[4,3,1024]{1,0,2:T(4,128)} copy(f32[4,3,1024]{2,1,0:T(4,128)S(1)} %all_gather.9) | data formatting | bytes 98304 | tf_op jit(solution)/shard_map/all_gather | solution.py:74
  32.4 9.7 %convolution_multiply_fusion = f32[1024,4,8]{2,1,0:T(4,128)S(1)} fusion(f32[4,3,1024]{1,0,2:T(4,128)} %copy.148, f32[8,3,1024]{1,0,2:T(8,128)} %copy.149), kind=kOutput, calls=%fused_computation | convolution fusion | flops 1212416 | bytes 278528 | tf_op jit(solution)/shard_map/jvp(scp,tcp->pst)/dot_general | solution.py:44
  42.1 0.9 copy.150
  43.0 0.2 reshape.78
  43.2 2.7 %add_multiply_fusion.3 = (f32[32,32,32]{1,0,2:T(8,128)S(1)}, f32[32,32,32]{1,0,2:T(8,128)S(1)}) fusion(f32[32,32,32]{1,2,0:T(8,128)S(1)} %get-tuple-element.40, f32[32,32,32]{1,2,0:T(8,128)S(1)} %get-tuple-element.41, f32[32,32,32]{1,0,2:T(8,128)S(1)} %reshape.78), kind=kLoop, calls=%fused_computation.116 | loop fusion | flops 589824 | bytes 655360 | tf_op jit(solution)/shard_map/jvp()/mul | solution.py:60
  45.9 0.7 add_multiply_fusion.11
  46.6 0.2 broadcast_multiply_fusion.3
  46.9 0.3 add_multiply_fusion.6
  47.2 0.3 add_rsqrt_fusion
  47.5 0.1 copy.165
  47.6 0.1 broadcast_bitcast_fusion.5
  47.7 3.3 %add_multiply_fusion.1 = (f32[32,32,32]{1,0,2:T(8,128)S(1)}, f32[32,32,32]{1,0,2:T(8,128)}) fusion(f32[32,32,32]{1,2,0:T(8,128)S(1)} %get-tuple-element.42, f32[32,32,32]{1,2,0:T(8,128)S(1)} %get-tuple-element.43, f32[32,32,32]{1,0,2:T(8,128)S(1)} %get-tuple-element.26), kind=kLoop, calls=%fused_computation.114 | loop fusion | flops 589824 | bytes 655360 | tf_op jit(solution)/shard_map/jvp()/mul | solution.py:60
  51.0 0.7 add_multiply_fusion.9
  51.7 0.8 broadcast_multiply_fusion.2
  52.6 0.3 add_multiply_fusion.5
  52.9 0.3 fusion.85
  53.2 0.1 copy.169
  53.3 0.1 broadcast_bitcast_fusion.3
  53.4 2.3 %multiply_reduce_fusion = (f32[32]{0:T(128)S(1)}, f32[32,32,32]{1,0,2:T(8,128)S(1)}) fusion(f32[32,32,32]{1,2,0:T(8,128)S(1)} %get-tuple-element.44, f32[32,32,32]{1,2,0:T(8,128)S(1)} %get-tuple-element.45, f32[32,32,32]{1,0,2:T(8,128)S(1)} %get-tuple-element.22), kind=kLoop, calls=%fused_computation.112 | loop fusion | flops 622560 | bytes 524416 | tf_op jit(solution)/shard_map/jvp()/reduce_sum | solution.py:65
  55.7 0.1 add.505
  55.7 0.2 fusion.155
  55.9 16.9 %psum.7 = f32[8,100]{1,0:T(8,128)S(1)} all-reduce(f32[8,100]{1,0:T(8,128)S(1)} %fusion.155), channel_id=1, replica_groups=mesh['tgt'=4,'sup'=8] {'sup'}, use_global_device_ids=true, to_apply=%region_3.4 | all-reduce | flops 800 | bytes 6400 | tf_op jit(solution)/shard_map/psum | solution.py:80
  72.8 8.6 %all-gather = f32[8,1,100]{2,1,0:T(1,128)S(1)} all-gather(f32[1,1,100]{2,1,0:T(1,128)S(1)} %bitcast.95), channel_id=1, replica_groups=mesh['tgt'=4,'sup'=8] {'sup'}, dimensions={0}, use_global_device_ids=true | all-gather | bytes 3600 | tf_op jit(solution)/shard_map/all_gather | solution.py:77
  81.4 0.1 fusion
  81.6 1.4 %fusion.35 = f32[32,32,4]{1,2,0:T(4,128)S(1)} fusion(f32[32,32,32]{1,0,2:T(8,128)S(1)} %get-tuple-element.19, f32[4,8]{1,0:T(4,128)S(1)} %fusion, f32[32,32,8]{1,2,0:T(8,128)S(1)} %copy.169, f32[32,32,4]{1,2,0:T(4,128)} %copy-done.16), kind=kLoop, calls=%fused_computation.84 | loop fusion | flops 323584 | bytes 196736 | tf_op jit(solution)/shard_map/transpose(jvp())/reduce_sum | solution.py:55
  83.0 0.9 fusion.144
  83.9 0.9 broadcast_bitcast_fusion.2
  84.8 0.1 broadcast_in_dim.16
  84.8 2.3 %fusion.47 = f32[32,32,32]{1,0,2:T(8,128)S(1)} fusion(f32[32,32,32]{1,2,0:T(8,128)} %broadcast_bitcast_fusion.2, f32[32,32,32]{1,2,0:T(8,128)S(1)} %get-tuple-element.44, f32[32]{0:T(128)S(1)} %broadcast_in_dim.16, f32[32,32,32]{1,0,2:T(8,128)S(1)} %get-tuple-element.19, f32[32,32,32]{1,2,0:T(8,128)S(1)} %get-tuple-element.45), kind=kLoop, calls=%fused_computation.105 | loop fusion | flops 294912 | bytes 655488 | tf_op jit(solution)/shard_map/transpose(jvp())/div | solution.py:23
  87.1 0.4 pad_add_fusion.2
  87.7 1.4 %fusion.46 = (f32[32,32,32]{1,0,2:T(8,128)S(1)}, f32[32,32,32]{1,0,2:T(8,128)S(1)}) fusion(f32[32,32,32]{1,2,0:T(8,128)S(1)} %broadcast_bitcast_fusion.1, f32[32,32,32]{1,2,0:T(8,128)S(1)} %copy-done.3, f32[32,32,32]{1,0,2:T(8,128)S(1)} %copy-done.1, f32[32,32,32]{1,2,0:T(8,128)S(1)} %copy-done.5, f32[32,32,32]{1,0,2:T(8,128)S(1)} %fusion.47, ...), kind=kLoop, calls=%fused_computation.103 | loop fusion | flops 524288 | bytes 1048576 | tf_op jit(solution)/shard_map/transpose(jvp())/div | solution.py:23
  89.1 0.4 pad_add_fusion.1
  89.7 1.5 %fusion.45 = (f32[32,32,32]{1,0,2:T(8,128)S(1)}, f32[32,32,32]{1,0,2:T(8,128)S(1)}) fusion(f32[32,32,32]{1,2,0:T(8,128)S(1)} %broadcast_bitcast_fusion, f32[32,32,32]{1,2,0:T(8,128)S(1)} %get-tuple-element.40, f32[32,32,32]{1,0,2:T(8,128)S(1)} %get-tuple-element.27, f32[32,32,32]{1,2,0:T(8,128)S(1)} %get-tuple-element.41, ...), kind=kLoop, calls=%fused_computation.101 | loop fusion | flops 524288 | bytes 1048576 | tf_op jit(solution)/shard_map/transpose(jvp())/div | solution.py:23
  91.2 0.8 fusion.43
  92.1 0.8 fusion.39
  92.9 0.1 pad_add_fusion.23
  93.0 0.2 fusion.100
  93.2 0.1 pad_add_fusion.22
  93.3 0.2 fusion.91
  93.5 0.1 pad_add_fusion.21
  93.6 0.2 fusion.139
  93.8 0.1 div.122
  93.8 0.4 pad_add_fusion
  94.3 0.8 fusion.31
  95.0 0.2 div.109
  95.3 1.1 copy.180
  96.4 11.1 %fusion.156 = f32[1024,4,3]{1,2,0:T(4,128)} fusion(f32[1024,4,8]{2,1,0:T(4,128)S(1)} %copy.180, f32[8,3,1024]{1,0,2:T(8,128)} %copy.149), kind=kOutput, calls=%fused_computation.323 | convolution fusion | flops 1179648 | bytes 278528 | tf_op jit(solution)/shard_map/transpose(jvp(scp,tcp->pst))/dot_general | solution.py:44
  107.5 1.8 %copy.182 = f32[1024,4,3]{0,1,2:T(4,128)S(1)} copy(f32[1024,4,3]{1,2,0:T(4,128)} %fusion.156) | data formatting | bytes 98304 | tf_op jit(solution)/shard_map/transpose(jvp(scp,tcp->pst))/dot_general | solution.py:44
  109.5 16.1 %all-reduce.63 = f32[4,3,1024]{2,1,0:T(4,128)S(1)} all-reduce(f32[4,3,1024]{2,1,0:T(4,128)S(1)} %copy.192), channel_id=2, replica_groups=mesh['tgt'=4,'sup'=8] {'tgt'}, use_global_device_ids=true, to_apply=%region_7.8.clone | all-reduce | flops 12288 | bytes 98304
  125.5 0.6 dynamic-slice
  126.1 0.7 constant_dynamic-slice_fusion
  126.8 0.6 copy.193
  127.4 0.5 constant_dynamic-slice_fusion.1
  (64 shorter events, 0.9 us)
Async XLA Ops:
  0.6 55.1 %copy-start = (f32[4,100]{1,0:T(4,128)S(1)}, f32[4,100]{1,0:T(4,128)}, u32[]{:S(2)}) copy-start(f32[4,100]{1,0:T(4,128)} %param.5) | copy-start | bytes 4804
  0.6 11.3 %copy-start.20 = (f32[1,3,1024]{2,0,1:T(1,128)S(1)}, f32[1,3,1024]{2,0,1:T(1,128)}, u32[]{:S(2)}) copy-start(f32[1,3,1024]{2,0,1:T(1,128)} %param.6) | copy-start | bytes 36868
  11.1 19.5 %copy-start.6 = (f32[4,3,1024]{2,1,0:T(4,128)}, f32[4,3,1024]{2,1,0:T(4,128)S(1)}, u32[]{:S(2)}) copy-start(f32[4,3,1024]{2,1,0:T(4,128)S(1)} %all_gather.9) | copy-start | bytes 147460
  11.9 34.0 %copy-start.8 = (f32[32,32,4]{1,0,2:T(8,128)}, f32[32,32,4]{1,0,2:T(8,128)S(1)}, u32[]{:S(2)}) copy-start(f32[32,32,4]{1,0,2:T(8,128)S(1)} %get-tuple-element.29) | copy-start | bytes 49156
  12.0 15.9 %copy-start.12 = (f32[32,32,4]{1,2,0:T(4,128)}, f32[32,32,4]{1,2,0:T(4,128)S(1)}, u32[]{:S(2)}) copy-start(f32[32,32,4]{1,2,0:T(4,128)S(1)} %copy.155) | copy-start | bytes 49156
  43.0 3.9 %copy-start.17 = (f32[32,32,8]{1,0,2:T(8,128)S(1)}, f32[32,32,8]{1,0,2:T(8,128)}, u32[]{:S(2)}) copy-start(f32[32,32,8]{1,0,2:T(8,128)} %get-tuple-element.31) | copy-start | bytes 98308
  46.8 4.2 %copy-start.10 = (f32[32,32,4]{1,0,2:T(8,128)}, f32[32,32,4]{1,0,2:T(8,128)S(1)}, u32[]{:S(2)}) copy-start(f32[32,32,4]{1,0,2:T(8,128)S(1)} %get-tuple-element.25) | copy-start | bytes 49156
  46.9 4.1 %copy-start.14 = (f32[32,32,4]{1,2,0:T(4,128)}, f32[32,32,4]{1,2,0:T(4,128)S(1)}, u32[]{:S(2)}) copy-start(f32[32,32,4]{1,2,0:T(4,128)S(1)} %copy.163) | copy-start | bytes 49156
  47.7 5.7 %copy-start.2 = (f32[32,32,32]{1,2,0:T(8,128)}, f32[32,32,32]{1,2,0:T(8,128)S(1)}, u32[]{:S(2)}) copy-start(f32[32,32,32]{1,2,0:T(8,128)S(1)} %get-tuple-element.42) | copy-start | bytes 393220
  47.7 5.7 %copy-start.4 = (f32[32,32,32]{1,2,0:T(8,128)}, f32[32,32,32]{1,2,0:T(8,128)S(1)}, u32[]{:S(2)}) copy-start(f32[32,32,32]{1,2,0:T(8,128)S(1)} %get-tuple-element.43) | copy-start | bytes 393220
  52.6 3.1 %copy-start.16 = (f32[32,32,4]{1,2,0:T(4,128)}, f32[32,32,4]{1,2,0:T(4,128)S(1)}, u32[]{:S(2)}) copy-start(f32[32,32,4]{1,2,0:T(4,128)S(1)} %copy.167) | copy-start | bytes 49156
  52.6 20.2 %copy-start.21 = (f32[1,100]{1,0:T(1,128)S(1)}, f32[1,100]{1,0:T(1,128)}, u32[]{:S(2)}) copy-start(f32[1,100]{1,0:T(1,128)} %param.7) | copy-start | bytes 1204
  83.9 3.6 %copy-start.19 = (f32[32,32,4]{1,0,2:T(8,128)S(1)}, f32[32,32,4]{1,0,2:T(8,128)}, u32[]{:S(2)}) copy-start(f32[32,32,4]{1,0,2:T(8,128)} %get-tuple-element.37) | copy-start | bytes 49156
  84.8 2.8 %copy-start.1 = (f32[32,32,32]{1,0,2:T(8,128)S(1)}, f32[32,32,32]{1,0,2:T(8,128)}, u32[]{:S(2)}) copy-start(f32[32,32,32]{1,0,2:T(8,128)} %get-tuple-element.23) | copy-start | bytes 393220
  84.8 2.8 %copy-start.3 = (f32[32,32,32]{1,2,0:T(8,128)S(1)}, f32[32,32,32]{1,2,0:T(8,128)}, u32[]{:S(2)}) copy-start(f32[32,32,32]{1,2,0:T(8,128)} %copy-done.2) | copy-start | bytes 393220
  84.8 2.8 %copy-start.5 = (f32[32,32,32]{1,2,0:T(8,128)S(1)}, f32[32,32,32]{1,2,0:T(8,128)}, u32[]{:S(2)}) copy-start(f32[32,32,32]{1,2,0:T(8,128)} %copy-done.4) | copy-start | bytes 393220
  87.7 1.9 %copy-start.18 = (f32[32,32,4]{1,0,2:T(8,128)S(1)}, f32[32,32,4]{1,0,2:T(8,128)}, u32[]{:S(2)}) copy-start(f32[32,32,4]{1,0,2:T(8,128)} %get-tuple-element.39) | copy-start | bytes 49156
  89.7 1.6 %copy-start.13 = (f32[32,32,4]{1,2,0:T(4,128)S(1)}, f32[32,32,4]{1,2,0:T(4,128)}, u32[]{:S(2)}) copy-start(f32[32,32,4]{1,2,0:T(4,128)} %copy-done.12) | copy-start | bytes 49156
  89.7 2.4 %copy-start.15 = (f32[32,32,4]{1,2,0:T(4,128)S(1)}, f32[32,32,4]{1,2,0:T(4,128)}, u32[]{:S(2)}) copy-start(f32[32,32,4]{1,2,0:T(4,128)} %copy-done.14) | copy-start | bytes 49156
  91.2 1.8 %copy-start.11 = (f32[32,32,4]{1,0,2:T(8,128)S(1)}, f32[32,32,4]{1,0,2:T(8,128)}, u32[]{:S(2)}) copy-start(f32[32,32,4]{1,0,2:T(8,128)} %copy-done.10) | copy-start | bytes 49156
  91.2 2.1 %copy-start.9 = (f32[32,32,4]{1,0,2:T(8,128)S(1)}, f32[32,32,4]{1,0,2:T(8,128)}, u32[]{:S(2)}) copy-start(f32[32,32,4]{1,0,2:T(8,128)} %copy-done.8) | copy-start | bytes 49156
  107.5 1.8 %copy-start.7 = (f32[4,3,1024]{2,1,0:T(4,128)S(1)}, f32[4,3,1024]{2,1,0:T(4,128)}, u32[]{:S(2)}) copy-start(f32[4,3,1024]{2,1,0:T(4,128)} %copy-done.6) | copy-start | bytes 147460
  107.5 18.0 %copy-start.22 = (u32[32]{0:T(128)S(1)}, u32[32]{0:T(128)}, u32[]{:S(2)}) copy-start(u32[32]{0:T(128)} %constant.232) | copy-start | bytes 388
where the time goes:
time: 128 us
  blocking collectives  65.5 us (51%)
  other arithmetic  25.1 us (20%)
  matrix products  21.2 us (17%)
  local copies, waits for them, and re-layouts  14.8 us (12%)
    dot_general x2, matrix products, pair_kernel(): jnp.einsum('scp,tcp->pst', support, targets, precision=lax.Precision.HIGH...  20.9 us
    psum x1, blocking collectives, local(): predicted = lax.psum(product(theta.T, coeffs), 'sup')  16.9 us
    unnamed x1, blocking collectives  16.1 us
    all_gather x1, blocking collectives, local(): lax.all_gather(targets, 'sup', axis=0, tiled=True)  14.3 us
    all_gather x1, blocking collectives, local(): block = lax.all_gather(support, 'tgt', axis=0, tiled=True)  9.71 us
    all_gather x1, blocking collectives, local(): lax.all_gather(labels, 'sup', axis=0, tiled=True)  8.65 us
    div x6, other arithmetic, spread(): return summed / 9.0  6.42 us
    mul x2, other arithmetic, pair_kernel(): activated = 2.0 / math.pi * jnp.arcsin(correlation)  6 us

commit v1 on v0

--- a/solution.py
+++ b/solution.py
@@ -1,3 +1,4 @@
+import functools
 import math
 import jax
 import jax.numpy as jnp
@@ -8,6 +9,33 @@
 DEPTH = 3
 WEIGHT_VAR = 1.6
 BIAS_VAR = 0.1
+
+
+def _assign_quarters(message, axis_tag, dimension_no):
+    kept_arr, w2, piece_out = (
+        lax.axis_size(axis_tag),
+        lax.axis_index(axis_tag),
+        message.shape[dimension_no],
+    )
+    pages = tuple(
+        (dd * kept_arr if ix == dimension_no else dd for ix, dd in enumerate(message.shape))
+    )
+    local_now = lax.dynamic_update_slice_in_dim(
+        jnp.zeros(pages, message.dtype), message, w2 * piece_out, axis=dimension_no
+    )
+    for m in range(1, kept_arr):
+        message = lax.ppermute(
+            message,
+            axis_name=axis_tag,
+            perm=tuple(((ix, (ix + 1) % kept_arr) for ix in range(kept_arr))),
+        )
+        local_now = lax.dynamic_update_slice_in_dim(
+            local_now, message, (w2 - m) % kept_arr * piece_out, axis=dimension_no
+        )
+    return local_now
+
+
+deliver_samples = functools.partial(_assign_quarters, axis_tag="sup", dimension_no=0)
 
 
 def spread(values):
@@ -73,7 +101,7 @@
     tgt_dev = targets.shape[0]
     block = lax.all_gather(support, "tgt", axis=0, tiled=True)
     group, group_labels = (
-        lax.all_gather(targets, "sup", axis=0, tiled=True),
+        deliver_samples(targets),
         lax.all_gather(labels, "sup", axis=0, tiled=True),
     )
     theta, pullback = jax.vjp(lambda images: pair_kernel(images, group), block)

time: 128 us -> 843 us (6.59)
  local copies, waits for them, and re-layouts: 14.8 us -> 654 us
  blocking collectives: 65.5 us -> 118 us
  waiting for transfers between devices: 0 us -> 21.7 us
    dynamic_update_slice x0 -> x8, local copies, waits for them, and re-layouts: none -> 621 us  [the longest x7 604 us: _assign_quarters(): lax.dynamic_update_slice_in_dim(local_now, message, (w2 - m) % kept_arr *...]
    all_gather x1, blocking collectives: 8.65 us -> 79 us  [local(): lax.all_gather(labels, 'sup', axis=0, tiled=True)]
    ppermute x0 -> x7, waiting for transfers between devices: none -> 21.7 us  [_assign_quarters(): lax.ppermute(message, axis_name=axis_tag, perm=tuple(((ix, (ix + 1) % kep...]
    all_gather x1 -> x0, blocking collectives: 14.3 us -> none  [local(): lax.all_gather(targets, 'sup', axis=0, tiled=True)]
    ppermute x0 -> x7, local copies, waits for them, and re-layouts: none -> 12.6 us  [_assign_quarters(): lax.ppermute(message, axis_name=axis_tag, perm=tuple(((ix, (ix + 1) % kep...]
  transfers between devices with their start and end apart: 0 -> 7, of which waited for: 0 -> 5; matrix products, arithmetic and copies ran while one was open for 0% -> 66% of each run, Pallas kernels for 0% -> 0%
where the time goes in v1:
time: 843 us; the launch traced here: 839 us
  local copies, waits for them, and re-layouts  654 us (78%)
  blocking collectives  118 us (14%)
  other arithmetic  24.9 us (3%)
  waiting for transfers between devices  21.7 us (3%)
  matrix products  18 us (2%)
    dynamic_update_slice x7, local copies, waits for them, and re-layouts, _assign_quarters(): lax.dynamic_update_slice_in_dim(local_now, message, (w2 - m) % kept_arr *...  604 us
    all_gather x1, blocking collectives, local(): lax.all_gather(labels, 'sup', axis=0, tiled=True)  79 us
    ppermute x7, waiting for transfers between devices, _assign_quarters(): lax.ppermute(message, axis_name=axis_tag, perm=tuple(((ix, (ix + 1) % kep...  21.7 us
    dot_general x2, matrix products, pair_kernel(): jnp.einsum('scp,tcp->pst', support, targets, precision=lax.Precision.HIGH...  17.7 us
    dynamic_update_slice x1, local copies, waits for them, and re-layouts, _assign_quarters(): lax.dynamic_update_slice_in_dim(jnp.zeros(pages, message.dtype), message,...  17.5 us
  transfers between devices with their start and end apart: 7, of which 5 were waited for; matrix products, arithmetic and copies ran while one was open for 66% of the time, Pallas kernels for 0%

profile of v1, /device:TPU:0, one launch (start us, length us, event | category | flops | bytes accessed | tf_op | source)
XLA Modules:
  0.0 838.8 jit_solution(8868835632556208092)
XLA Ops:
  0.6 0.5 collective-permute-start
  1.2 0.7 copy.183
  1.9 9.2 %all_gather.6 = f32[4,3,1024]{2,1,0:T(4,128)S(1)} all-gather(f32[1,3,1024]{2,1,0:T(4,128)S(1)} %copy.183), channel_id=1, replica_groups=mesh['tgt'=4,'sup'=8] {'tgt'}, dimensions={0}, use_global_device_ids=true | all-gather | bytes 61440 | tf_op jit(solution)/shard_map/all_gather | solution.py:102
  11.5 0.3 copy.225
  12.1 0.5 copy-done.18
  12.8 4.2 collective-permute-done.1
  17.2 4.7 collective-permute-done.2
  22.1 4.7 collective-permute-done.3
  26.8 0.9 broadcast_bitcast_fusion.1
  27.7 4.0 collective-permute-done.4
  31.7 0.9 broadcast_bitcast_fusion
  32.6 4.0 collective-permute-done.5
  36.7 0.8 broadcast_multiply_fusion.2
  37.5 1.7 copy.175
  39.2 1.7 copy.184
  40.9 0.7 copy.190
  41.6 0.7 copy.195
  42.2 0.7 copy.199
  42.9 0.6 dynamic-slice
  43.7 17.5 %dynamic_update_slice.24 = f32[8,3,1024]{0,1,2:T(4,128)S(1)} dynamic-update-slice(f32[8,3,1024]{0,1,2:T(4,128)S(1)} %broadcast_in_dim.19, f32[1,3,1024]{0,1,2:T(4,128)} %copy.175, s32[]{:T(128)S(6)} %select_n.56, s32[]{:T(128)} %constant.136.clone.1, s32[]{:T(128)} %constant.136.clone.1) | dynamic-update-slice | bytes 24580 | tf_op jit(solution)/shard_map/dynamic_update_slice | solution.py:23
  61.2 79.0 %all-gather = f32[8,1,100]{2,1,0:T(1,128)S(1)} all-gather(f32[1,1,100]{2,1,0:T(1,128)S(1)} %bitcast.97), channel_id=1, replica_groups=mesh['tgt'=4,'sup'=8] {'sup'}, dimensions={0}, use_global_device_ids=true | all-gather | bytes 3600 | tf_op jit(solution)/shard_map/all_gather | solution.py:105
  140.2 2.2 copy.176
  142.4 86.3 %dynamic_update_slice.25 = f32[8,3,1024]{0,1,2:T(4,128)S(1)} dynamic-update-slice(f32[8,3,1024]{0,1,2:T(4,128)S(1)} %dynamic_update_slice.24, f32[1,3,1024]{0,1,2:T(4,128)} %copy.176, s32[]{:T(128)S(6)} %select_n.58, s32[]{:T(128)} %constant.136.clone.1, s32[]{:T(128)} %constant.136.clone.1) | dynamic-update-slice | bytes 24580 | tf_op jit(solution)/shard_map/dynamic_update_slice | solution.py:32
  228.7 1.7 copy.177
  230.4 86.3 %dynamic_update_slice.26 = f32[8,3,1024]{0,1,2:T(4,128)S(1)} dynamic-update-slice(f32[8,3,1024]{0,1,2:T(4,128)S(1)} %dynamic_update_slice.25, f32[1,3,1024]{0,1,2:T(4,128)} %copy.177, s32[]{:T(128)S(6)} %select_n.60, s32[]{:T(128)} %constant.136.clone.1, s32[]{:T(128)} %constant.136.clone.1) | dynamic-update-slice | bytes 24580 | tf_op jit(solution)/shard_map/dynamic_update_slice | solution.py:32
  316.7 1.7 copy.178
  318.4 86.3 %dynamic_update_slice.27 = f32[8,3,1024]{0,1,2:T(4,128)S(1)} dynamic-update-slice(f32[8,3,1024]{0,1,2:T(4,128)S(1)} %dynamic_update_slice.26, f32[1,3,1024]{0,1,2:T(4,128)} %copy.178, s32[]{:T(128)S(6)} %select_n.62, s32[]{:T(128)} %constant.136.clone.1, s32[]{:T(128)} %constant.136.clone.1) | dynamic-update-slice | bytes 24580 | tf_op jit(solution)/shard_map/dynamic_update_slice | solution.py:32
  404.7 1.7 copy.179
  406.4 86.3 %dynamic_update_slice.28 = f32[8,3,1024]{0,1,2:T(4,128)S(1)} dynamic-update-slice(f32[8,3,1024]{0,1,2:T(4,128)S(1)} %dynamic_update_slice.27, f32[1,3,1024]{0,1,2:T(4,128)} %copy.179, s32[]{:T(128)S(6)} %select_n.64, s32[]{:T(128)} %constant.136.clone.1, s32[]{:T(128)} %constant.136.clone.1) | dynamic-update-slice | bytes 24580 | tf_op jit(solution)/shard_map/dynamic_update_slice | solution.py:32
  492.7 1.7 copy.180
  494.4 86.3 %dynamic_update_slice.29 = f32[8,3,1024]{0,1,2:T(4,128)S(1)} dynamic-update-slice(f32[8,3,1024]{0,1,2:T(4,128)S(1)} %dynamic_update_slice.28, f32[1,3,1024]{0,1,2:T(4,128)} %copy.180, s32[]{:T(128)S(6)} %select_n.66, s32[]{:T(128)} %constant.136.clone.1, s32[]{:T(128)} %constant.136.clone.1) | dynamic-update-slice | bytes 24580 | tf_op jit(solution)/shard_map/dynamic_update_slice | solution.py:32
  580.7 1.7 copy.181
  582.4 86.3 %dynamic_update_slice.30 = f32[8,3,1024]{0,1,2:T(4,128)S(1)} dynamic-update-slice(f32[8,3,1024]{0,1,2:T(4,128)S(1)} %dynamic_update_slice.29, f32[1,3,1024]{0,1,2:T(4,128)} %copy.181, s32[]{:T(128)S(6)} %select_n.68, s32[]{:T(128)} %constant.136.clone.1, s32[]{:T(128)} %constant.136.clone.1) | dynamic-update-slice | bytes 24580 | tf_op jit(solution)/shard_map/dynamic_update_slice | solution.py:32
  668.7 1.7 copy.182
  670.4 86.3 %dynamic_update_slice.31 = f32[8,3,1024]{0,1,2:T(4,128)S(1)} dynamic-update-slice(f32[8,3,1024]{0,1,2:T(4,128)S(1)} %dynamic_update_slice.30, f32[1,3,1024]{0,1,2:T(4,128)} %copy.182, s32[]{:T(128)S(6)} %select_n.70, s32[]{:T(128)} %constant.136.clone.1, s32[]{:T(128)} %constant.136.clone.1) | dynamic-update-slice | bytes 24580 | tf_op jit(solution)/shard_map/dynamic_update_slice | solution.py:32
  756.7 1.5 multiply_reduce_fusion
  758.3 8.4 multiply_bitcast_fusion
  766.6 1.8 copy.185
  768.5 1.0 reshape.78
  770.1 0.3 add_multiply_fusion.6
  770.8 0.3 add_multiply_fusion.5
  771.8 0.3 copy-done.13
  772.1 3.3 add_multiply_fusion.3
  775.4 3.3 add_multiply_fusion.1
  778.7 2.8 multiply_reduce_fusion.1
  781.9 13.8 %psum.7 = f32[8,100]{1,0:T(8,128)S(1)} all-reduce(f32[8,100]{1,0:T(8,128)S(1)} %fusion.154), channel_id=1, replica_groups=mesh['tgt'=4,'sup'=8] {'sup'}, use_global_device_ids=true, to_apply=%region_3.4 | all-reduce | flops 800 | bytes 6400 | tf_op jit(solution)/shard_map/psum | solution.py:108
  795.8 0.5 constant_dynamic-slice_fusion.1
  796.4 1.7 fusion.35
  798.1 0.9 fusion.143
  799.1 0.9 fusion.47
  800.1 0.4 pad_add_fusion.2
  800.5 1.4 fusion.46
  802.0 0.4 pad_add_fusion.1
  802.5 1.4 fusion.45
  803.9 0.8 fusion.43
  804.8 0.8 fusion.39
  806.6 0.4 pad_add_fusion
  807.0 0.8 fusion.31
  808.0 2.0 copy.212
  810.0 9.3 %fusion.155 = f32[1024,4,3]{1,2,0:T(4,128)} fusion(f32[1024,4,8]{2,1,0:T(4,128)} %copy.212, f32[8,3,1024]{0,1,2:T(4,128)S(1)} %dynamic_update_slice.31), kind=kOutput, calls=%fused_computation.322 | convolution fusion | flops 1179648 | bytes 278528 | tf_op jit(solution)/shard_map/transpose(jvp(scp,tcp->pst))/dot_general | solution.py:72
  819.3 1.8 copy.213
  821.2 16.0 %all-reduce.63 = f32[4,3,1024]{2,1,0:T(4,128)S(1)} all-reduce(f32[4,3,1024]{2,1,0:T(4,128)S(1)} %copy.223), channel_id=2, replica_groups=mesh['tgt'=4,'sup'=8] {'tgt'}, use_global_device_ids=true, to_apply=%region_7.8.clone | all-reduce | flops 12288 | bytes 98304
  837.3 0.7 constant_dynamic-slice_fusion
  837.9 0.6 copy.224
  (105 shorter events, 5.1 us)
Async XLA Ops:
  0.6 781.1 %copy-start = (f32[4,100]{1,0:T(4,128)S(1)}, f32[4,100]{1,0:T(4,128)}, u32[]{:S(2)}) copy-start(f32[4,100]{1,0:T(4,128)} %param.5) | copy-start | bytes 4804
  0.6 11.4 %collective-permute-start = (f32[1,3,1024]{2,0,1:T(1,128)}, f32[1,3,1024]{2,0,1:T(1,128)S(1)}, u32[]{:S(2)}, u32[]{:S(2)}) collective-permute-start(f32[1,3,1024]{2,0,1:T(1,128)} %param.6), channel_id=1, source_target_pairs={{0,1},{1,2},{2,3},{3,4},{4,5},{5,6},{6,7},{7,0},{8,9},{9,10},{10,1... | collective-permute-start | bytes 36872 | tf_op jit(solution)/shard_map/ppermute | solution.py:27
  11.1 28.0 %copy-start.16 = (f32[4,3,1024]{2,1,0:T(4,128)}, f32[4,3,1024]{2,1,0:T(4,128)S(1)}, u32[]{:S(2)}) copy-start(f32[4,3,1024]{2,1,0:T(4,128)S(1)} %all_gather.6) | copy-start | bytes 147460
  11.4 26.0 %copy-start.27 = (f32[1,3,1024]{2,0,1:T(1,128)S(1)}, f32[1,3,1024]{2,0,1:T(1,128)}, u32[]{:S(2)}) copy-start(f32[1,3,1024]{2,0,1:T(1,128)} %param.6) | copy-start | bytes 36868
  12.0 0.6 copy-start.18
  12.0 5.0 collective-permute-start.1
  17.0 4.9 collective-permute-start.2
  17.2 4.7 copy-start.20
  21.9 4.9 collective-permute-start.3
  26.8 4.9 collective-permute-start.4
  31.7 4.9 collective-permute-start.5
  36.7 632.0 %collective-permute-start.6 = (f32[1,3,1024]{2,0,1:T(1,128)S(1)}, f32[1,3,1024]{2,0,1:T(1,128)S(1)}, u32[]{:S(2)}, u32[]{:S(2)}) collective-permute-start(f32[1,3,1024]{2,0,1:T(1,128)S(1)} %collective-permute-done.5), channel_id=1, source_target_pairs={{0,1},{1,2},{2,3},{3,4},{4,5},{5,6},{6,7},{7,0},{8,9},{9,10},{10,1... | collective-permute-start | bytes 36872 | tf_op jit(solution)/shard_map/ppermute | solution.py:27
  37.5 5.4 copy-start.29
  43.7 17.5 %copy-start.28 = (f32[1,100]{1,0:T(1,128)S(1)}, f32[1,100]{1,0:T(1,128)}, u32[]{:S(2)}) copy-start(f32[1,100]{1,0:T(1,128)} %param.7) | copy-start | bytes 1204
  756.7 1.6 copy-start.1
  769.5 2.0 copy-start.24
  769.5 2.1 copy-start.22
  770.1 1.6 copy-start.26
  771.1 1.0 copy-start.13
  771.6 3.9 copy-start.3
  771.6 3.8 copy-start.5
  771.7 7.0 copy-start.9
  771.7 7.0 copy-start.11
  796.4 2.7 copy-start.2
  799.0 1.5 copy-start.7
  799.0 1.5 copy-start.10
  799.0 1.5 copy-start.12
  799.0 1.5 copy-start.14
  800.5 1.9 copy-start.4
  800.5 1.9 copy-start.6
  800.5 1.9 copy-start.8
  800.5 1.9 copy-start.15
  802.4 1.5 copy-start.25
  802.5 2.3 copy-start.23
  803.9 1.8 copy-start.21
  803.9 2.1 copy-start.19
  819.3 1.8 copy-start.17
